TPU v7x, 256 devices: a whole 4x4x8 slice. The times are simulated.
256 devices in a mesh: blk: 128 (over z, y, x), chan: 2 (over core).
Axes of the slice: x: 4, y: 4, z: 8, core: 2. Of those that a mesh axis runs over, the one named last changes fastest.
Arguments:
- inputs: bfloat16 [128, 512, 512], P('chan', 'blk'), may hold values from -6 to 6
- w_first: bfloat16 [3, 3, 128, 128], P(None, None, 'chan'), may hold values from -0.1875 to 0.1875
- w_second: bfloat16 [3, 3, 128, 128], P(None, None, 'chan'), may hold values from -0.1875 to 0.1875
- w_third: bfloat16 [3, 3, 256, 128], P(None, None, 'chan'), may hold values from -0.1875 to 0.1875
- cotangent: bfloat16 [256, 256, 256], P('chan', 'blk'), may hold values from -6 to 6
- mirror: int32 [128], P('blk'), may hold values from 0 to 1
Outputs:
- grad_inputs: bfloat16 [128, 512, 512], P('chan', 'blk')
- grad_first: float32 [3, 3, 128, 128], P(None, None, 'chan')
- grad_second: float32 [3, 3, 128, 128], P(None, None, 'chan')
- grad_third: float32 [3, 3, 256, 128], P(None, None, 'chan')
Inputs may be any that keep to these rules, and one draw needn't show every extreme that they name: `mirror`: 1 marks a tile whose columns are stored in reverse order, 0 a tile stored in the cycle's order.
All inputs are finite; a program needn't handle non-finite values.
Results may differ from a plain program's by a relative error of at most 0.024.
Values may be sent and summed in bfloat16 or wider, within the bound.
A program may use at most 64 MiB of HBM per device.

v0:
```python
import math
import jax
import jax.numpy as jnp
from jax import lax
from jax.sharding import PartitionSpec as P


def extended(shard, sides, width):
    for axis, dim in sides:
        devices, length = (lax.axis_size(axis), shard.shape[dim])
        up = [(i, (i + 1) % devices) for i in range(devices)]
        down = [(j, i) for i, j in up]
        last = lax.slice_in_dim(shard, length - width, length, axis=dim)
        leading = lax.slice_in_dim(shard, 0, width, axis=dim)
        before = lax.ppermute(last, axis, up)
        after = lax.ppermute(leading, axis, down)
        shard = jnp.concatenate([before, shard, after], axis=dim)
    return shard


def passed_along(shard, axis, by):
    devices = lax.axis_size(axis)
    return lax.ppermute(shard, axis, [(i, (i + by) % devices) for i in range(devices)])


def orient(block, mirrored):
    return jnp.where(mirrored == 1, block[..., ::-1], block)


def widen(active):
    gathered = lax.all_gather(active, "chan", axis=0, tiled=True)
    return extended(gathered, (("blk", 1),), 1)


def widen_by(active, before_rows, after_rows):
    gathered = lax.all_gather(active, "chan", axis=0, tiled=True)
    devices, length = (lax.axis_size("blk"), gathered.shape[1])
    up = [(i, (i + 1) % devices) for i in range(devices)]
    down = [(j, i) for i, j in up]
    before = lax.ppermute(gathered[:, length - before_rows :], "blk", up)
    after = lax.ppermute(gathered[:, :after_rows], "blk", down)
    return jnp.concatenate([before, gathered, after], axis=1)


def conv_taps(padded, weight):
    row_count = padded.shape[1] - 2
    col_count = padded.shape[2]
    framed = jnp.pad(padded, ((0, 0), (0, 0), (1, 1)))
    running = jnp.zeros((weight.shape[2], row_count, col_count), jnp.float32)
    for row_tap in range(3):
        for col_tap in range(3):
            running = running + jnp.einsum(
                "oi,irw->orw",
                weight[row_tap, col_tap],
                framed[:, row_tap : row_tap + row_count, col_tap : col_tap + col_count],
                preferred_element_type=jnp.float32,
            )
    return running


def weight_taps(grad_out, padded):
    row_count = grad_out.shape[1]
    col_count = grad_out.shape[2]
    framed = jnp.pad(padded, ((0, 0), (0, 0), (1, 1)))
    views = jnp.stack(
        [
            framed[:, row_tap : row_tap + row_count, col_tap : col_tap + col_count]
            for row_tap in range(3)
            for col_tap in range(3)
        ]
    )
    taps = jnp.einsum("orw,kirw->koi", grad_out, views, preferred_element_type=jnp.float32)
    return taps.reshape((3, 3) + taps.shape[1:])


def spread_taps(grad_out, weight):
    row_count = grad_out.shape[1]
    col_count = grad_out.shape[2]
    framed = jnp.pad(grad_out, ((0, 0), (2, 2), (2, 2)))
    running = jnp.zeros((weight.shape[3], row_count + 2, col_count), jnp.float32)
    for row_tap in range(3):
        for col_tap in range(3):
            row_start = 2 - row_tap
            col_start = 3 - col_tap
            running = running + jnp.einsum(
                "oi,orw->irw",
                weight[row_tap, col_tap],
                framed[:, row_start : row_start + row_count + 2, col_start : col_start + col_count],
                preferred_element_type=jnp.float32,
            )
    return running


def spread_stride(grad_out, weight):
    out_rows = grad_out.shape[1]
    out_cols = grad_out.shape[2]
    channels = weight.shape[3]
    framed = jnp.pad(grad_out, ((0, 0), (1, 1), (1, 1)))
    parity_rows = []
    for row_par in range(2):
        parity_cols = []
        for col_par in range(2):
            running = jnp.zeros((channels, out_rows + 1, out_cols + 1), jnp.float32)
            for row_tap in range(row_par, 3, 2):
                for col_tap in range(col_par, 3, 2):
                    row_start = 1 - row_tap // 2
                    col_start = 1 - col_tap // 2
                    running = running + jnp.einsum(
                        "oi,orw->irw",
                        weight[row_tap, col_tap],
                        framed[
                            :,
                            row_start : row_start + out_rows + 1,
                            col_start : col_start + out_cols + 1,
                        ],
                        preferred_element_type=jnp.float32,
                    )
            parity_cols.append(running)
        parity_rows.append(jnp.stack(parity_cols, axis=3))
    woven = jnp.stack(parity_rows, axis=2)
    woven = woven.reshape(channels, 2 * out_rows + 2, 2 * out_cols + 2)
    return woven[:, : 2 * out_rows + 1, 1 : 2 * out_cols + 1]


def fold_rims(grad_rows, both_sides):
    interior = grad_rows[:, 1:-1] if both_sides else grad_rows[:, 1:]
    from_next = passed_along(grad_rows[:, :1].astype(jnp.bfloat16), "blk", -1).astype(jnp.float32)
    if both_sides:
        from_prev = passed_along(grad_rows[:, -1:].astype(jnp.bfloat16), "blk", 1).astype(
            jnp.float32
        )
        return jnp.concatenate(
            [interior[:, :1] + from_prev, interior[:, 1:-1], interior[:, -1:] + from_next], axis=1
        )
    return jnp.concatenate([interior[:, :-1], interior[:, -1:] + from_next], axis=1)


def own_inputs(weight):
    whole = lax.all_gather(weight, "chan", axis=2, tiled=True)
    width = whole.shape[3] // lax.axis_size("chan")
    return lax.dynamic_slice_in_dim(whole, lax.axis_index("chan") * width, width, axis=3)


def input_grad(delta, weight):
    every = lax.all_gather(delta, "chan", axis=0, tiled=True)
    return fold_rims(spread_taps(every, weight), True)


def third_input_grad(upstream, weight):
    every = lax.all_gather(upstream, "chan", axis=0, tiled=True)
    return fold_rims(spread_stride(every, weight), False)


def parity_picker(cols, out_cols):
    source = lax.broadcasted_iota(jnp.int32, (cols, 3 * out_cols), 0)
    target = lax.broadcasted_iota(jnp.int32, (cols, 3 * out_cols), 1)
    wanted = 2 * (target % out_cols) + target // out_cols - 1
    return (source == wanted).astype(jnp.bfloat16)


def summed_over_cycle(parts, axis):
    devices = lax.axis_size(axis)
    flat = jnp.concatenate([p.reshape(-1) for p in parts])
    pieces = lax.all_to_all(flat.reshape(devices, -1), axis, 0, 0, tiled=True)
    total = jnp.sum(pieces, axis=0)
    spread = jnp.broadcast_to(total[None], (devices,) + total.shape)
    whole = lax.all_to_all(spread, axis, 0, 0, tiled=True).reshape(-1)
    out, start = ([], 0)
    for p in parts:
        out.append(whole[start : start + p.size].reshape(p.shape))
        start += p.size
    return out


def gelu_back(pre_act, grad_in):
    return jax.vjp(jax.nn.gelu, pre_act)[1](grad_in)[0]


def shards(inputs, w_first, w_second, w_third, cotangent, mirror):
    mirrored = mirror[0]
    oriented = orient(inputs, mirrored)
    upstream = orient(cotangent, mirrored)
    first_wide = widen_by(oriented, 3, 2)
    first_pre_wide = conv_taps(first_wide, w_first)
    first_act_wide = jax.nn.gelu(first_pre_wide).astype(jnp.bfloat16)
    first_pad = first_wide[:, 2:-1]
    first_pre = first_pre_wide[:, 2:-1]
    second_wide = lax.all_gather(first_act_wide, "chan", axis=0, tiled=True)
    second_pre_wide = conv_taps(second_wide, w_second)
    second_act_wide = jax.nn.gelu(second_pre_wide).astype(jnp.bfloat16)
    second_pad = second_wide[:, 1:]
    second_pre = second_pre_wide[:, 1:]
    stride_rows = lax.all_gather(second_act_wide, "chan", axis=0, tiled=True)
    out_rows = upstream.shape[1]
    out_cols = upstream.shape[2]
    by_parity = jnp.einsum(
        "irt,tk->irk",
        stride_rows,
        parity_picker(2 * out_cols, out_cols),
        preferred_element_type=jnp.float32,
    ).astype(jnp.bfloat16)
    spaced = jnp.stack([upstream, jnp.zeros_like(upstream)], axis=2).reshape(
        upstream.shape[0], 2 * out_rows, out_cols
    )
    row_placed = jnp.stack(
        [
            jnp.pad(spaced, ((0, 0), (row_tap, 1), (0, 0)))[:, : 2 * out_rows + 1]
            for row_tap in range(3)
        ]
    )
    third_grad = jnp.stack(
        [
            jnp.einsum(
                "aosc,isc->aoi",
                row_placed,
                by_parity[:, :, col_tap * out_cols : (col_tap + 1) * out_cols],
                preferred_element_type=jnp.float32,
            )
            for col_tap in range(3)
        ],
        axis=1,
    )
    second_back = third_input_grad(upstream, own_inputs(w_third))
    second_delta = gelu_back(second_pre, second_back).astype(jnp.bfloat16)
    second_grad = weight_taps(second_delta, second_pad)
    first_back = input_grad(second_delta, own_inputs(w_second))
    first_delta = gelu_back(first_pre, first_back).astype(jnp.bfloat16)
    first_grad = weight_taps(first_delta, first_pad)
    input_back = input_grad(first_delta, own_inputs(w_first)).astype(jnp.bfloat16)
    reduced = summed_over_cycle((first_grad, second_grad, third_grad), "blk")
    cell_count = inputs.shape[1] * inputs.shape[2] * lax.axis_size("blk")
    return (
        orient(input_back, mirrored),
        reduced[0] / math.sqrt(cell_count),
        reduced[1] / math.sqrt(cell_count),
        reduced[2] / math.sqrt(cell_count // 4),
    )


def solution(mesh):
    placed = (
        P("chan", "blk", None),
        P(None, None, "chan", None),
        P(None, None, "chan", None),
        P(None, None, "chan", None),
        P("chan", "blk", None),
        P("blk"),
    )
    return jax.shard_map(
        shards,
        mesh=mesh,
        in_specs=placed,
        out_specs=(
            P("chan", "blk", None),
            P(None, None, "chan", None),
            P(None, None, "chan", None),
            P(None, None, "chan", None),
        ),
        check_vma=False,
    )
```

profile of v0, /device:TPU:8, one launch (start us, length us, event | category | flops | bytes accessed | tf_op | source)
XLA Modules:
  0.0 161.4 jit_solution(18438336296300883969)
XLA Ops:
  1.3 1.0 copy.69
  2.3 0.5 rev.10
  2.8 1.0 broadcast_select_fusion.1
  3.9 2.3 %all_gather.31 = bf16[128,4,512]{2,0,1:T(8,128)(2,1)S(1)} all-gather(bf16[64,4,512]{2,0,1:T(8,128)(2,1)S(1)} %broadcast_select_fusion.1), channel_id=1, replica_groups=mesh['blk'=128,'chan'=2] {'chan'}, dimensions={0}, use_global_device_ids=true | all-gather | bytes 786432 | tf_op jit(solution)/shard_map/all_gather | solution.py:36
  6.2 0.8 slice.569
  7.0 1.5 collective-permute-start.1
  8.4 0.7 slice.570
  9.2 2.6 %collective-permute-start.2 = (bf16[128,2,512]{2,0,1:T(8,128)(2,1)}, bf16[128,2,512]{2,0,1:T(8,128)(2,1)}, u32[]{:S(2)}, u32[]{:S(2)}) collective-permute-start(bf16[128,2,512]{2,0,1:T(8,128)(2,1)} %slice.570), channel_id=1, source_target_pairs={{2,0},{4,2},{6,4},{8,6},{10,8},{12,10},{14,12},{16,14},{18,16},{20... | collective-permute-start | bytes 786440 | tf_op jit(solution)/shard_map/ppermute | solution.py:41
  12.2 2.0 %all_gather.30 = bf16[256,2,256]{0,2,1:T(8,128)(2,1)S(1)} all-gather(bf16[128,2,256]{0,2,1:T(8,128)(2,1)S(1)} %broadcast_select_fusion.2), channel_id=1, replica_groups=mesh['blk'=128,'chan'=2] {'chan'}, dimensions={0}, use_global_device_ids=true | all-gather | bytes 393216 | tf_op jit(solution)/shard_map/all_gather | solution.py:150
  14.4 2.2 %all_gather.29 = bf16[3,3,256,128]{2,3,1,0:T(8,128)(2,1)S(1)} all-gather(bf16[3,3,128,128]{2,3,1,0:T(8,128)(2,1)S(1)} %copy.62), channel_id=1, replica_groups=mesh['blk'=128,'chan'=2] {'chan'}, dimensions={2}, use_global_device_ids=true | all-gather | bytes 884736 | tf_op jit(solution)/shard_map/all_gather | solution.py:139
  19.0 1.1 copy.65
  20.1 2.3 %reshape.51 = f32[64,6,514]{0,2,1:T(8,128)} reshape(f32[64,3,2,257,2]{0,4,3,2,1:T(2,128)S(1)} %copy.65) | data formatting | bytes 1579008 | tf_op jit(solution)/shard_map/reshape | solution.py:121
  22.4 1.0 slice.568
  23.5 0.6 collective-permute-start
  24.1 1.2 slice.566
  25.3 1.0 slice.567
  27.2 2.0 %all_gather.28 = bf16[3,3,128,128]{3,2,1,0:T(8,128)(2,1)S(1)} all-gather(bf16[3,3,64,128]{3,2,1,0:T(8,128)(2,1)S(1)} %copy-done), channel_id=1, replica_groups=mesh['blk'=128,'chan'=2] {'chan'}, dimensions={2}, use_global_device_ids=true | all-gather | bytes 442368 | tf_op jit(solution)/shard_map/all_gather | solution.py:139
  29.2 1.1 constant_dynamic-update-slice_fusion.4
  30.4 1.0 constant_dynamic-update-slice_fusion
  31.5 0.5 fusion.18
  32.0 0.5 fusion.19
  32.4 0.5 fusion.20
  32.9 0.5 fusion.21
  33.4 0.5 fusion.22
  34.7 0.9 fusion.30
  35.5 2.6 %all_gather.32 = bf16[128,7,512]{2,0,1:T(8,128)(2,1)S(1)} all-gather(bf16[64,7,512]{2,0,1:T(8,128)(2,1)S(1)} %get-tuple-element.41), channel_id=1, replica_groups=mesh['blk'=128,'chan'=2] {'chan'}, dimensions={0}, use_global_device_ids=true | all-gather | bytes 1376256 | tf_op jit(solution)/shard_map/all_gather | solution.py:188
  38.9 0.4 convolution_add_fusion.23
  39.3 0.4 convolution_add_fusion.22
  41.0 0.5 fusion.52
  41.5 2.3 %all_gather.35 = bf16[128,5,512]{2,0,1:T(8,128)(2,1)S(1)} all-gather(bf16[64,5,512]{2,0,1:T(8,128)(2,1)S(1)} %get-tuple-element.47), channel_id=1, replica_groups=mesh['blk'=128,'chan'=2] {'chan'}, dimensions={0}, use_global_device_ids=true | all-gather | bytes 983040 | tf_op jit(solution)/shard_map/all_gather | solution.py:193
  43.8 0.7 fusion.3
  44.5 0.4 convolution_bitcast_fusion.1
  44.9 0.4 convolution_bitcast_fusion.2
  45.4 0.4 convolution_bitcast_fusion.3
  47.6 2.2 %all_gather.33 = bf16[128,4,512]{2,0,1:T(8,128)(2,1)S(1)} all-gather(bf16[64,4,512]{2,0,1:T(8,128)(2,1)S(1)} %fusion.63), channel_id=1, replica_groups=mesh['blk'=128,'chan'=2] {'chan'}, dimensions={0}, use_global_device_ids=true | all-gather | bytes 786432 | tf_op jit(solution)/shard_map/all_gather | solution.py:145
  49.8 0.4 fusion.35
  50.6 0.4 convolution_add_fusion.15
  51.0 0.4 convolution_add_fusion.14
  51.8 0.4 convolution_add_fusion.12
  53.4 1.6 collective-permute-start.3
  55.0 2.6 %collective-permute-start.4 = (bf16[64,1,512]{2,0,1:T(8,128)(2,1)S(1)}, bf16[64,1,512]{2,0,1:T(8,128)(2,1)S(1)}, u32[]{:S(2)}, u32[]{:S(2)}) collective-permute-start(bf16[64,1,512]{2,0,1:T(8,128)(2,1)S(1)} %get-tuple-element.35), channel_id=1, source_target_pairs={{0,254},{2,0},{4,2},{6,4},{8,6},{10,8},{12,10},{14,12},{16,14},{18... | collective-permute-start | bytes 196616 | tf_op jit(solution)/shard_map/ppermute | solution.py:23
  59.4 1.5 fusion.103
  61.1 0.9 fusion.99
  62.7 1.5 fusion.105
  64.2 1.1 pad_maximum_fusion.1
  65.4 19.3 %all-to-all-start = ((f32[128,1,2304]{2,1,0:T(1,128)}), f32[128,1,2304]{2,1,0:T(1,128)S(1)}, u32[]{:S(2)}, u32[]{:S(2)}) async-start(f32[128,1,2304]{2,1,0:T(1,128)} %bitcast.146), calls=%async_computation | async-start | bytes 2359296 | tf_op jit(solution)/shard_map/all_to_all | solution.py:164
  84.7 2.0 %all_gather.27 = bf16[3,3,128,128]{3,2,1,0:T(8,128)(2,1)S(1)} all-gather(bf16[3,3,64,128]{3,2,1,0:T(8,128)(2,1)S(1)} %copy-done.1), channel_id=1, replica_groups=mesh['blk'=128,'chan'=2] {'chan'}, dimensions={2}, use_global_device_ids=true | all-gather | bytes 442368 | tf_op jit(solution)/shard_map/all_gather | solution.py:139
  86.7 2.2 %all_gather.34 = bf16[128,4,512]{2,0,1:T(8,128)(2,1)S(1)} all-gather(bf16[64,4,512]{2,0,1:T(8,128)(2,1)S(1)} %fusion.70), channel_id=1, replica_groups=mesh['blk'=128,'chan'=2] {'chan'}, dimensions={0}, use_global_device_ids=true | all-gather | bytes 786432 | tf_op jit(solution)/shard_map/all_gather | solution.py:145
  88.9 0.4 fusion.36
  89.6 0.4 convolution_add_fusion.7
  90.1 27.3 %all-to-all-done = f32[128,1,2304]{2,1,0:T(1,128)S(1)} async-done(((f32[128,1,2304]{2,1,0:T(1,128)}), f32[128,1,2304]{2,1,0:T(1,128)S(1)}, u32[]{:S(2)}, u32[]{:S(2)}) %all-to-all-start) | async-done | bytes 1179680 | tf_op jit(solution)/shard_map/all_to_all | solution.py:164
  117.4 0.7 reduce_sum.9
  118.1 1.7 %broadcast_in_dim.2 = f32[128,1,2304]{2,1,0:T(1,128)} broadcast(f32[2304]{0:T(1024)S(1)} %reduce_sum.9), dimensions={2} | broadcast | bytes 1188864 | tf_op jit(solution)/shard_map/broadcast_in_dim | solution.py:166
  119.7 6.3 %all-to-all-start.1 = ((f32[128,1,2304]{2,1,0:T(1,128)}), f32[128,1,2304]{2,1,0:T(1,128)S(1)}, u32[]{:S(2)}, u32[]{:S(2)}) async-start(f32[128,1,2304]{2,1,0:T(1,128)} %broadcast_in_dim.2), calls=%async_computation.1 | async-start | bytes 2359296 | tf_op jit(solution)/shard_map/all_to_all | solution.py:167
  126.1 0.4 convolution_add_fusion.6
  126.9 0.4 convolution_add_fusion.4
  128.5 1.8 %collective-permute-start.5 = (bf16[64,1,512]{2,0,1:T(8,128)(2,1)S(1)}, bf16[64,1,512]{2,0,1:T(8,128)(2,1)S(1)}, u32[]{:S(2)}, u32[]{:S(2)}) collective-permute-start(bf16[64,1,512]{2,0,1:T(8,128)(2,1)S(1)} %get-tuple-element.32), channel_id=1, source_target_pairs={{0,2},{2,4},{4,6},{6,8},{8,10},{10,12},{12,14},{14,16},{16,18},{18... | collective-permute-start | bytes 196616 | tf_op jit(solution)/shard_map/ppermute | solution.py:23
  130.3 2.7 %collective-permute-start.6 = (bf16[64,1,512]{2,0,1:T(8,128)(2,1)S(1)}, bf16[64,1,512]{2,0,1:T(8,128)(2,1)S(1)}, u32[]{:S(2)}, u32[]{:S(2)}) collective-permute-start(bf16[64,1,512]{2,0,1:T(8,128)(2,1)S(1)} %get-tuple-element.33), channel_id=1, source_target_pairs={{0,254},{2,0},{4,2},{6,4},{8,6},{10,8},{12,10},{14,12},{16,14},{18... | collective-permute-start | bytes 196616 | tf_op jit(solution)/shard_map/ppermute | solution.py:23
  133.0 3.0 %collective-permute-done.5 = bf16[64,1,512]{2,0,1:T(8,128)(2,1)S(1)} collective-permute-done((bf16[64,1,512]{2,0,1:T(8,128)(2,1)S(1)}, bf16[64,1,512]{2,0,1:T(8,128)(2,1)S(1)}, u32[]{:S(2)}, u32[]{:S(2)}) %collective-permute-start.5) | collective-permute-done | bytes 65568 | tf_op jit(solution)/shard_map/ppermute | solution.py:23
  136.0 0.5 rev.11
  136.6 0.9 copy.74
  137.5 21.2 %all-to-all-done.1 = f32[128,1,2304]{2,1,0:T(1,128)S(1)} async-done(((f32[128,1,2304]{2,1,0:T(1,128)}), f32[128,1,2304]{2,1,0:T(1,128)S(1)}, u32[]{:S(2)}, u32[]{:S(2)}) %all-to-all-start.1) | async-done | bytes 1179680 | tf_op jit(solution)/shard_map/all_to_all | solution.py:167
  158.7 1.4 slice_multiply_fusion.1
  160.1 1.3 slice_multiply_fusion
  (90 shorter events, 14.9 us)
Async XLA Ops:
  2.8 9.0 %copy-start.3 = (bf16[128,2,256]{2,1,0:T(2,128)(2,1)S(1)}, bf16[128,2,256]{2,1,0:T(2,128)(2,1)}, u32[]{:S(2)}) copy-start(bf16[128,2,256]{2,1,0:T(2,128)(2,1)} %param.10) | copy-start | bytes 393220
  3.9 10.3 %copy-start.2 = (bf16[3,3,128,128]{3,2,1,0:T(8,128)(2,1)S(1)}, bf16[3,3,128,128]{3,2,1,0:T(8,128)(2,1)}, u32[]{:S(2)}) copy-start(bf16[3,3,128,128]{3,2,1,0:T(8,128)(2,1)} %param.9) | copy-start | bytes 884740
  7.0 22.3 %collective-permute-start.1 = (bf16[128,3,512]{2,0,1:T(8,128)(2,1)}, bf16[128,3,512]{2,0,1:T(8,128)(2,1)}, u32[]{:S(2)}, u32[]{:S(2)}) collective-permute-start(bf16[128,3,512]{2,0,1:T(8,128)(2,1)} %slice.569), channel_id=1, source_target_pairs={{0,2},{2,4},{4,6},{6,8},{8,10},{10,12},{12,14},{14,16},{16,18},{18... | collective-permute-start | bytes 1179656 | tf_op jit(solution)/shard_map/ppermute | solution.py:40
  9.2 21.3 %collective-permute-start.2 = (bf16[128,2,512]{2,0,1:T(8,128)(2,1)}, bf16[128,2,512]{2,0,1:T(8,128)(2,1)}, u32[]{:S(2)}, u32[]{:S(2)}) collective-permute-start(bf16[128,2,512]{2,0,1:T(8,128)(2,1)} %slice.570), channel_id=1, source_target_pairs={{2,0},{4,2},{6,4},{8,6},{10,8},{12,10},{14,12},{16,14},{18,16},{20... | collective-permute-start | bytes 786440 | tf_op jit(solution)/shard_map/ppermute | solution.py:41
  23.5 5.7 %collective-permute-start = (bf16[64,1,512]{2,0,1:T(8,128)(2,1)S(1)}, bf16[64,1,512]{2,0,1:T(8,128)(2,1)S(1)}, u32[]{:S(2)}, u32[]{:S(2)}) collective-permute-start(bf16[64,1,512]{2,0,1:T(8,128)(2,1)S(1)} %copy.104), channel_id=1, source_target_pairs={{0,254},{2,0},{4,2},{6,4},{8,6},{10,8},{12,10},{14,12},{16,14},{18... | collective-permute-start | bytes 196616 | tf_op jit(solution)/shard_map/ppermute | solution.py:23
  26.3 0.9 copy-start
  30.3 1.2 copy-start.1
  53.4 8.8 %collective-permute-start.3 = (bf16[64,1,512]{2,0,1:T(8,128)(2,1)S(1)}, bf16[64,1,512]{2,0,1:T(8,128)(2,1)S(1)}, u32[]{:S(2)}, u32[]{:S(2)}) collective-permute-start(bf16[64,1,512]{2,0,1:T(8,128)(2,1)S(1)} %get-tuple-element.34), channel_id=1, source_target_pairs={{0,2},{2,4},{4,6},{6,8},{8,10},{10,12},{12,14},{14,16},{16,18},{18... | collective-permute-start | bytes 196616 | tf_op jit(solution)/shard_map/ppermute | solution.py:23
  55.0 7.3 %collective-permute-start.4 = (bf16[64,1,512]{2,0,1:T(8,128)(2,1)S(1)}, bf16[64,1,512]{2,0,1:T(8,128)(2,1)S(1)}, u32[]{:S(2)}, u32[]{:S(2)}) collective-permute-start(bf16[64,1,512]{2,0,1:T(8,128)(2,1)S(1)} %get-tuple-element.35), channel_id=1, source_target_pairs={{0,254},{2,0},{4,2},{6,4},{8,6},{10,8},{12,10},{14,12},{16,14},{18... | collective-permute-start | bytes 196616 | tf_op jit(solution)/shard_map/ppermute | solution.py:23
  65.4 52.0 %all-to-all-start = ((f32[128,1,2304]{2,1,0:T(1,128)}), f32[128,1,2304]{2,1,0:T(1,128)S(1)}, u32[]{:S(2)}, u32[]{:S(2)}) async-start(f32[128,1,2304]{2,1,0:T(1,128)} %bitcast.146), calls=%async_computation | async-start | bytes 2359296 | tf_op jit(solution)/shard_map/all_to_all | solution.py:164
  119.7 39.0 %all-to-all-start.1 = ((f32[128,1,2304]{2,1,0:T(1,128)}), f32[128,1,2304]{2,1,0:T(1,128)S(1)}, u32[]{:S(2)}, u32[]{:S(2)}) async-start(f32[128,1,2304]{2,1,0:T(1,128)} %broadcast_in_dim.2), calls=%async_computation.1 | async-start | bytes 2359296 | tf_op jit(solution)/shard_map/all_to_all | solution.py:167
  128.5 7.5 %collective-permute-start.5 = (bf16[64,1,512]{2,0,1:T(8,128)(2,1)S(1)}, bf16[64,1,512]{2,0,1:T(8,128)(2,1)S(1)}, u32[]{:S(2)}, u32[]{:S(2)}) collective-permute-start(bf16[64,1,512]{2,0,1:T(8,128)(2,1)S(1)} %get-tuple-element.32), channel_id=1, source_target_pairs={{0,2},{2,4},{4,6},{6,8},{8,10},{10,12},{12,14},{14,16},{16,18},{18... | collective-permute-start | bytes 196616 | tf_op jit(solution)/shard_map/ppermute | solution.py:23
  130.3 5.7 %collective-permute-start.6 = (bf16[64,1,512]{2,0,1:T(8,128)(2,1)S(1)}, bf16[64,1,512]{2,0,1:T(8,128)(2,1)S(1)}, u32[]{:S(2)}, u32[]{:S(2)}) collective-permute-start(bf16[64,1,512]{2,0,1:T(8,128)(2,1)S(1)} %get-tuple-element.33), channel_id=1, source_target_pairs={{0,254},{2,0},{4,2},{6,4},{8,6},{10,8},{12,10},{14,12},{16,14},{18... | collective-permute-start | bytes 196616 | tf_op jit(solution)/shard_map/ppermute | solution.py:23
where the time goes:
time: 162 us; the launch traced here: 161 us
  waiting for transfers between devices  51.5 us (32%)
  starting transfers between devices  39.1 us (24%)
  matrix products  21.5 us (13%)
  local copies, waits for them, and re-layouts  19.8 us (12%)
  blocking collectives  19.8 us (12%)
  other arithmetic  7.65 us (5%)
  between operations  2.11 us (1%)
    all_to_all x1, waiting for transfers between devices, summed_over_cycle(): pieces = lax.all_to_all(flat.reshape(devices, -1), axis, 0, 0, tiled=True)  27.3 us
    all_to_all x1, waiting for transfers between devices, summed_over_cycle(): whole = lax.all_to_all(spread, axis, 0, 0, tiled=True).reshape(-1)  21.2 us
    all_to_all x1, starting transfers between devices, summed_over_cycle(): pieces = lax.all_to_all(flat.reshape(devices, -1), axis, 0, 0, tiled=True)  19.3 us
    ppermute x5, starting transfers between devices, passed_along(): lax.ppermute(shard, axis, [(i, (i + by) % devices) for i in range(devices)])  9.3 us
    dot_general x18, matrix products, conv_taps(): jnp.einsum('oi,irw->orw', weight[row_tap, col_tap], framed[:, row_tap:row...  7.17 us
    dot_general x18, matrix products, spread_taps(): jnp.einsum('oi,orw->irw', weight[row_tap, col_tap], framed[:, row_start:r...  7.11 us
    unnamed x32, local copies, waits for them, and re-layouts  7.02 us
    all_to_all x1, starting transfers between devices, summed_over_cycle(): whole = lax.all_to_all(spread, axis, 0, 0, tiled=True).reshape(-1)  6.34 us
  transfers between devices with their start and end apart: 9, of which 3 were waited for; matrix products, arithmetic and copies ran while one was open for 13% of the time, Pallas kernels for 0%

commit v1 on v0

--- a/solution.py
+++ b/solution.py
@@ -142,7 +142,9 @@
 
 
 def input_grad(delta, weight):
-    every = lax.all_gather(delta, "chan", axis=0, tiled=True)
+    every = jnp.concatenate(
+        lax.all_to_all(jnp.stack([delta] * lax.axis_size("chan")), "chan", 0, 0), axis=0
+    )
     return fold_rims(spread_taps(every, weight), True)
 
 

time: 162 us -> 171 us (1.056)
  waiting for transfers between devices: 51.5 us -> 56.3 us
  starting transfers between devices: 39.1 us -> 42.5 us
    all_gather x2 -> x0, blocking collectives: 4.35 us -> none  [input_grad(): every = lax.all_gather(delta, 'chan', axis=0, tiled=True)]
    all_to_all x0 -> x1, blocking collectives: none -> 4.15 us  [input_grad(): lax.all_to_all(jnp.stack([delta] * lax.axis_size('chan')), 'chan', 0, 0)]
    all_to_all x1, waiting for transfers between devices: 27.3 us -> 30.9 us  [summed_over_cycle(): pieces = lax.all_to_all(flat.reshape(devices, -1), axis, 0, 0, tiled=True)]
    all_to_all x0 -> x1, starting transfers between devices: none -> 3.49 us  [input_grad(): lax.all_to_all(jnp.stack([delta] * lax.axis_size('chan')), 'chan', 0, 0)]
  transfers between devices with their start and end apart: 9 -> 10, of which waited for: 3 -> 4; matrix products, arithmetic and copies ran while one was open for 13% -> 13% of each run, Pallas kernels for 0% -> 0%
where the time goes in v1:
time: 171 us; the launch traced here: 170 us
  waiting for transfers between devices  56.3 us (33%)
  starting transfers between devices  42.5 us (25%)
  matrix products  21.5 us (13%)
  local copies, waits for them, and re-layouts  19.8 us (12%)
  blocking collectives  19.6 us (11%)
  other arithmetic  8.49 us (5%)
  between operations  2.13 us (1%)
    all_to_all x1, waiting for transfers between devices, summed_over_cycle(): pieces = lax.all_to_all(flat.reshape(devices, -1), axis, 0, 0, tiled=True)  30.9 us
    all_to_all x1, waiting for transfers between devices, summed_over_cycle(): whole = lax.all_to_all(spread, axis, 0, 0, tiled=True).reshape(-1)  21.3 us
    all_to_all x1, starting transfers between devices, summed_over_cycle(): pieces = lax.all_to_all(flat.reshape(devices, -1), axis, 0, 0, tiled=True)  19.3 us
    ppermute x5, starting transfers between devices, passed_along(): lax.ppermute(shard, axis, [(i, (i + by) % devices) for i in range(devices)])  9.3 us
    dot_general x18, matrix products, conv_taps(): jnp.einsum('oi,irw->orw', weight[row_tap, col_tap], framed[:, row_tap:row...  7.17 us
    dot_general x18, matrix products, spread_taps(): jnp.einsum('oi,orw->irw', weight[row_tap, col_tap], framed[:, row_start:r...  7.12 us
    unnamed x32, local copies, waits for them, and re-layouts  7.02 us
    all_to_all x1, starting transfers between devices, summed_over_cycle(): whole = lax.all_to_all(spread, axis, 0, 0, tiled=True).reshape(-1)  6.34 us
  transfers between devices with their start and end apart: 10, of which 4 were waited for; matrix products, arithmetic and copies ran while one was open for 13% of the time, Pallas kernels for 0%

profile of v1, /device:TPU:8, one launch (start us, length us, event | category | flops | bytes accessed | tf_op | source)
XLA Modules:
  0.0 170.4 jit_solution(7247264507438603536)
XLA Ops:
  1.3 1.0 copy.75
  2.3 0.5 rev.10
  2.8 1.0 broadcast_select_fusion.1
  3.9 2.3 %all_gather.25 = bf16[128,4,512]{2,0,1:T(8,128)(2,1)S(1)} all-gather(bf16[64,4,512]{2,0,1:T(8,128)(2,1)S(1)} %broadcast_select_fusion.1), channel_id=1, replica_groups=mesh['blk'=128,'chan'=2] {'chan'}, dimensions={0}, use_global_device_ids=true | all-gather | bytes 786432 | tf_op jit(solution)/shard_map/all_gather | solution.py:36
  6.2 0.8 slice.569
  7.0 1.5 collective-permute-start.1
  8.4 0.7 slice.570
  9.2 2.6 %collective-permute-start.2 = (bf16[128,2,512]{2,0,1:T(8,128)(2,1)}, bf16[128,2,512]{2,0,1:T(8,128)(2,1)}, u32[]{:S(2)}, u32[]{:S(2)}) collective-permute-start(bf16[128,2,512]{2,0,1:T(8,128)(2,1)} %slice.570), channel_id=1, source_target_pairs={{2,0},{4,2},{6,4},{8,6},{10,8},{12,10},{14,12},{16,14},{18,16},{20... | collective-permute-start | bytes 786440 | tf_op jit(solution)/shard_map/ppermute | solution.py:41
  12.2 2.0 %all_gather.24 = bf16[256,2,256]{0,2,1:T(8,128)(2,1)S(1)} all-gather(bf16[128,2,256]{0,2,1:T(8,128)(2,1)S(1)} %broadcast_select_fusion.2), channel_id=1, replica_groups=mesh['blk'=128,'chan'=2] {'chan'}, dimensions={0}, use_global_device_ids=true | all-gather | bytes 393216 | tf_op jit(solution)/shard_map/all_gather | solution.py:152
  14.4 2.2 %all_gather.23 = bf16[3,3,256,128]{2,3,1,0:T(8,128)(2,1)S(1)} all-gather(bf16[3,3,128,128]{2,3,1,0:T(8,128)(2,1)S(1)} %copy.68), channel_id=1, replica_groups=mesh['blk'=128,'chan'=2] {'chan'}, dimensions={2}, use_global_device_ids=true | all-gather | bytes 884736 | tf_op jit(solution)/shard_map/all_gather | solution.py:139
  19.0 1.1 copy.71
  20.1 2.3 %reshape.57 = f32[64,6,514]{0,2,1:T(8,128)} reshape(f32[64,3,2,257,2]{0,4,3,2,1:T(2,128)S(1)} %copy.71) | data formatting | bytes 1579008 | tf_op jit(solution)/shard_map/reshape | solution.py:121
  22.4 1.0 slice.568
  23.5 0.6 collective-permute-start
  24.1 1.2 slice.566
  25.3 1.0 slice.567
  27.2 2.0 %all_gather.22 = bf16[3,3,128,128]{3,2,1,0:T(8,128)(2,1)S(1)} all-gather(bf16[3,3,64,128]{3,2,1,0:T(8,128)(2,1)S(1)} %copy-done), channel_id=1, replica_groups=mesh['blk'=128,'chan'=2] {'chan'}, dimensions={2}, use_global_device_ids=true | all-gather | bytes 442368 | tf_op jit(solution)/shard_map/all_gather | solution.py:139
  29.2 1.1 constant_dynamic-update-slice_fusion.4
  30.4 1.0 constant_dynamic-update-slice_fusion
  31.5 0.5 fusion.18
  32.0 0.5 fusion.19
  32.4 0.5 fusion.20
  32.9 0.5 fusion.21
  33.4 0.5 fusion.22
  34.7 0.9 fusion.30
  35.5 2.6 %all_gather.26 = bf16[128,7,512]{2,0,1:T(8,128)(2,1)S(1)} all-gather(bf16[64,7,512]{2,0,1:T(8,128)(2,1)S(1)} %get-tuple-element.41), channel_id=1, replica_groups=mesh['blk'=128,'chan'=2] {'chan'}, dimensions={0}, use_global_device_ids=true | all-gather | bytes 1376256 | tf_op jit(solution)/shard_map/all_gather | solution.py:190
  41.0 0.5 fusion.52
  41.5 2.3 %all_gather.27 = bf16[128,5,512]{2,0,1:T(8,128)(2,1)S(1)} all-gather(bf16[64,5,512]{2,0,1:T(8,128)(2,1)S(1)} %get-tuple-element.47), channel_id=1, replica_groups=mesh['blk'=128,'chan'=2] {'chan'}, dimensions={0}, use_global_device_ids=true | all-gather | bytes 983040 | tf_op jit(solution)/shard_map/all_gather | solution.py:195
  43.8 0.7 fusion.3
  44.5 0.4 convolution_bitcast_fusion.1
  44.9 0.4 convolution_bitcast_fusion.2
  45.4 0.4 convolution_bitcast_fusion.3
  47.7 4.2 %all_to_all.25 = bf16[2,64,4,512]{3,1,2,0:T(8,128)(2,1)S(1)} all-to-all(bf16[2,64,4,512]{3,1,2,0:T(8,128)(2,1)S(1)} %pad_maximum_fusion.6), channel_id=1, replica_groups=mesh['blk'=128,'chan'=2] {'chan'}, dimensions={0} | all-to-all | bytes 1048576 | tf_op jit(solution)/shard_map/all_to_all | solution.py:146
  51.9 0.4 fusion.35
  52.6 0.4 convolution_add_fusion.15
  53.1 0.4 convolution_add_fusion.14
  53.9 0.4 convolution_add_fusion.12
  55.5 1.6 collective-permute-start.3
  57.1 2.6 %collective-permute-start.4 = (bf16[64,1,512]{2,0,1:T(8,128)(2,1)S(1)}, bf16[64,1,512]{2,0,1:T(8,128)(2,1)S(1)}, u32[]{:S(2)}, u32[]{:S(2)}) collective-permute-start(bf16[64,1,512]{2,0,1:T(8,128)(2,1)S(1)} %get-tuple-element.35), channel_id=1, source_target_pairs={{0,254},{2,0},{4,2},{6,4},{8,6},{10,8},{12,10},{14,12},{16,14},{18... | collective-permute-start | bytes 196616 | tf_op jit(solution)/shard_map/ppermute | solution.py:23
  61.5 1.5 fusion.103
  63.1 0.9 fusion.99
  64.8 1.5 fusion.105
  66.3 0.8 pad_maximum_fusion.8
  67.1 3.5 %all-to-all-start.1 = ((bf16[2,64,4,512]{3,1,2,0:T(8,128)(2,1)}), bf16[2,64,4,512]{3,1,2,0:T(8,128)(2,1)S(1)}, u32[]{:S(2)}, u32[]{:S(2)}) async-start(bf16[2,64,4,512]{3,1,2,0:T(8,128)(2,1)} %pad_maximum_fusion.8), calls=%async_computation.1 | async-start | bytes 1048576 | tf_op jit(solution)/shard_map/all_to_all | solution.py:146
  70.6 1.1 pad_maximum_fusion.1
  71.7 0.6 all-to-all-done.1
  72.4 19.3 %all-to-all-start.2 = ((f32[128,1,2304]{2,1,0:T(1,128)}), f32[128,1,2304]{2,1,0:T(1,128)S(1)}, u32[]{:S(2)}, u32[]{:S(2)}) async-start(f32[128,1,2304]{2,1,0:T(1,128)} %bitcast.150), calls=%async_computation.2 | async-start | bytes 2359296 | tf_op jit(solution)/shard_map/all_to_all | solution.py:166
  91.7 2.0 %all_gather.21 = bf16[3,3,128,128]{3,2,1,0:T(8,128)(2,1)S(1)} all-gather(bf16[3,3,64,128]{3,2,1,0:T(8,128)(2,1)S(1)} %copy-done.1), channel_id=1, replica_groups=mesh['blk'=128,'chan'=2] {'chan'}, dimensions={2}, use_global_device_ids=true | all-gather | bytes 442368 | tf_op jit(solution)/shard_map/all_gather | solution.py:139
  93.7 0.4 fusion.36
  94.5 0.4 convolution_add_fusion.7
  94.9 30.9 %all-to-all-done.2 = f32[128,1,2304]{2,1,0:T(1,128)S(1)} async-done(((f32[128,1,2304]{2,1,0:T(1,128)}), f32[128,1,2304]{2,1,0:T(1,128)S(1)}, u32[]{:S(2)}, u32[]{:S(2)}) %all-to-all-start.2) | async-done | bytes 1179680 | tf_op jit(solution)/shard_map/all_to_all | solution.py:166
  125.8 0.7 reduce_sum.9
  126.5 1.6 broadcast_in_dim.2
  128.1 6.3 %all-to-all-start.3 = ((f32[128,1,2304]{2,1,0:T(1,128)}), f32[128,1,2304]{2,1,0:T(1,128)S(1)}, u32[]{:S(2)}, u32[]{:S(2)}) async-start(f32[128,1,2304]{2,1,0:T(1,128)} %broadcast_in_dim.2), calls=%async_computation.3 | async-start | bytes 2359296 | tf_op jit(solution)/shard_map/all_to_all | solution.py:169
  134.4 0.4 convolution_add_fusion.6
  135.3 0.4 convolution_add_fusion.4
  136.9 1.8 %collective-permute-start.5 = (bf16[64,1,512]{2,0,1:T(8,128)(2,1)S(1)}, bf16[64,1,512]{2,0,1:T(8,128)(2,1)S(1)}, u32[]{:S(2)}, u32[]{:S(2)}) collective-permute-start(bf16[64,1,512]{2,0,1:T(8,128)(2,1)S(1)} %get-tuple-element.32), channel_id=1, source_target_pairs={{0,2},{2,4},{4,6},{6,8},{8,10},{10,12},{12,14},{14,16},{16,18},{18... | collective-permute-start | bytes 196616 | tf_op jit(solution)/shard_map/ppermute | solution.py:23
  138.7 2.7 %collective-permute-start.6 = (bf16[64,1,512]{2,0,1:T(8,128)(2,1)S(1)}, bf16[64,1,512]{2,0,1:T(8,128)(2,1)S(1)}, u32[]{:S(2)}, u32[]{:S(2)}) collective-permute-start(bf16[64,1,512]{2,0,1:T(8,128)(2,1)S(1)} %get-tuple-element.33), channel_id=1, source_target_pairs={{0,254},{2,0},{4,2},{6,4},{8,6},{10,8},{12,10},{14,12},{16,14},{18... | collective-permute-start | bytes 196616 | tf_op jit(solution)/shard_map/ppermute | solution.py:23
  141.4 3.5 %collective-permute-done.5 = bf16[64,1,512]{2,0,1:T(8,128)(2,1)S(1)} collective-permute-done((bf16[64,1,512]{2,0,1:T(8,128)(2,1)S(1)}, bf16[64,1,512]{2,0,1:T(8,128)(2,1)S(1)}, u32[]{:S(2)}, u32[]{:S(2)}) %collective-permute-start.5) | collective-permute-done | bytes 65568 | tf_op jit(solution)/shard_map/ppermute | solution.py:23
  144.9 0.5 rev.11
  145.5 0.9 copy.82
  146.4 21.3 %all-to-all-done.3 = f32[128,1,2304]{2,1,0:T(1,128)S(1)} async-done(((f32[128,1,2304]{2,1,0:T(1,128)}), f32[128,1,2304]{2,1,0:T(1,128)S(1)}, u32[]{:S(2)}, u32[]{:S(2)}) %all-to-all-start.3) | async-done | bytes 1179680 | tf_op jit(solution)/shard_map/all_to_all | solution.py:169
  167.7 1.4 slice_multiply_fusion.1
  169.1 1.3 slice_multiply_fusion
  (95 shorter events, 15.8 us)
Async XLA Ops:
  2.8 9.0 %copy-start.3 = (bf16[128,2,256]{2,1,0:T(2,128)(2,1)S(1)}, bf16[128,2,256]{2,1,0:T(2,128)(2,1)}, u32[]{:S(2)}) copy-start(bf16[128,2,256]{2,1,0:T(2,128)(2,1)} %param.10) | copy-start | bytes 393220
  3.9 10.3 %copy-start.2 = (bf16[3,3,128,128]{3,2,1,0:T(8,128)(2,1)S(1)}, bf16[3,3,128,128]{3,2,1,0:T(8,128)(2,1)}, u32[]{:S(2)}) copy-start(bf16[3,3,128,128]{3,2,1,0:T(8,128)(2,1)} %param.9) | copy-start | bytes 884740
  7.0 22.3 %collective-permute-start.1 = (bf16[128,3,512]{2,0,1:T(8,128)(2,1)}, bf16[128,3,512]{2,0,1:T(8,128)(2,1)}, u32[]{:S(2)}, u32[]{:S(2)}) collective-permute-start(bf16[128,3,512]{2,0,1:T(8,128)(2,1)} %slice.569), channel_id=1, source_target_pairs={{0,2},{2,4},{4,6},{6,8},{8,10},{10,12},{12,14},{14,16},{16,18},{18... | collective-permute-start | bytes 1179656 | tf_op jit(solution)/shard_map/ppermute | solution.py:40
  9.2 21.2 %collective-permute-start.2 = (bf16[128,2,512]{2,0,1:T(8,128)(2,1)}, bf16[128,2,512]{2,0,1:T(8,128)(2,1)}, u32[]{:S(2)}, u32[]{:S(2)}) collective-permute-start(bf16[128,2,512]{2,0,1:T(8,128)(2,1)} %slice.570), channel_id=1, source_target_pairs={{2,0},{4,2},{6,4},{8,6},{10,8},{12,10},{14,12},{16,14},{18,16},{20... | collective-permute-start | bytes 786440 | tf_op jit(solution)/shard_map/ppermute | solution.py:41
  23.5 5.7 %collective-permute-start = (bf16[64,1,512]{2,0,1:T(8,128)(2,1)S(1)}, bf16[64,1,512]{2,0,1:T(8,128)(2,1)S(1)}, u32[]{:S(2)}, u32[]{:S(2)}) collective-permute-start(bf16[64,1,512]{2,0,1:T(8,128)(2,1)S(1)} %copy.112), channel_id=1, source_target_pairs={{0,254},{2,0},{4,2},{6,4},{8,6},{10,8},{12,10},{14,12},{16,14},{18... | collective-permute-start | bytes 196616 | tf_op jit(solution)/shard_map/ppermute | solution.py:23
  26.3 0.9 copy-start
  30.3 1.2 copy-start.1
  55.5 8.8 %collective-permute-start.3 = (bf16[64,1,512]{2,0,1:T(8,128)(2,1)S(1)}, bf16[64,1,512]{2,0,1:T(8,128)(2,1)S(1)}, u32[]{:S(2)}, u32[]{:S(2)}) collective-permute-start(bf16[64,1,512]{2,0,1:T(8,128)(2,1)S(1)} %get-tuple-element.34), channel_id=1, source_target_pairs={{0,2},{2,4},{4,6},{6,8},{8,10},{10,12},{12,14},{14,16},{16,18},{18... | collective-permute-start | bytes 196616 | tf_op jit(solution)/shard_map/ppermute | solution.py:23
  57.1 7.3 %collective-permute-start.4 = (bf16[64,1,512]{2,0,1:T(8,128)(2,1)S(1)}, bf16[64,1,512]{2,0,1:T(8,128)(2,1)S(1)}, u32[]{:S(2)}, u32[]{:S(2)}) collective-permute-start(bf16[64,1,512]{2,0,1:T(8,128)(2,1)S(1)} %get-tuple-element.35), channel_id=1, source_target_pairs={{0,254},{2,0},{4,2},{6,4},{8,6},{10,8},{12,10},{14,12},{16,14},{18... | collective-permute-start | bytes 196616 | tf_op jit(solution)/shard_map/ppermute | solution.py:23
  67.1 5.2 %all-to-all-start.1 = ((bf16[2,64,4,512]{3,1,2,0:T(8,128)(2,1)}), bf16[2,64,4,512]{3,1,2,0:T(8,128)(2,1)S(1)}, u32[]{:S(2)}, u32[]{:S(2)}) async-start(bf16[2,64,4,512]{3,1,2,0:T(8,128)(2,1)} %pad_maximum_fusion.8), calls=%async_computation.1 | async-start | bytes 1048576 | tf_op jit(solution)/shard_map/all_to_all | solution.py:146
  72.4 53.4 %all-to-all-start.2 = ((f32[128,1,2304]{2,1,0:T(1,128)}), f32[128,1,2304]{2,1,0:T(1,128)S(1)}, u32[]{:S(2)}, u32[]{:S(2)}) async-start(f32[128,1,2304]{2,1,0:T(1,128)} %bitcast.150), calls=%async_computation.2 | async-start | bytes 2359296 | tf_op jit(solution)/shard_map/all_to_all | solution.py:166
  128.1 39.6 %all-to-all-start.3 = ((f32[128,1,2304]{2,1,0:T(1,128)}), f32[128,1,2304]{2,1,0:T(1,128)S(1)}, u32[]{:S(2)}, u32[]{:S(2)}) async-start(f32[128,1,2304]{2,1,0:T(1,128)} %broadcast_in_dim.2), calls=%async_computation.3 | async-start | bytes 2359296 | tf_op jit(solution)/shard_map/all_to_all | solution.py:169
  136.9 8.0 %collective-permute-start.5 = (bf16[64,1,512]{2,0,1:T(8,128)(2,1)S(1)}, bf16[64,1,512]{2,0,1:T(8,128)(2,1)S(1)}, u32[]{:S(2)}, u32[]{:S(2)}) collective-permute-start(bf16[64,1,512]{2,0,1:T(8,128)(2,1)S(1)} %get-tuple-element.32), channel_id=1, source_target_pairs={{0,2},{2,4},{4,6},{6,8},{8,10},{10,12},{12,14},{14,16},{16,18},{18... | collective-permute-start | bytes 196616 | tf_op jit(solution)/shard_map/ppermute | solution.py:23
  138.7 6.2 %collective-permute-start.6 = (bf16[64,1,512]{2,0,1:T(8,128)(2,1)S(1)}, bf16[64,1,512]{2,0,1:T(8,128)(2,1)S(1)}, u32[]{:S(2)}, u32[]{:S(2)}) collective-permute-start(bf16[64,1,512]{2,0,1:T(8,128)(2,1)S(1)} %get-tuple-element.33), channel_id=1, source_target_pairs={{0,254},{2,0},{4,2},{6,4},{8,6},{10,8},{12,10},{14,12},{16,14},{18... | collective-permute-start | bytes 196616 | tf_op jit(solution)/shard_map/ppermute | solution.py:23
